TPU v7x, 256 devices: a whole 4x4x8 slice. The times are simulated.
256 devices in a mesh: panel: 4 (over x), front: 64 (over y, z, core).
Axes of the slice: x: 4, y: 4, z: 8, core: 2. Of those that a mesh axis runs over, the one named last changes fastest.
Arguments:
- top_source: bfloat16 [4, 128, 4096], P('panel', None, 'front'), may hold values from -6 to 6
- leaf_source: bfloat16 [4, 128, 589824], P('panel', None, 'front'), may hold values from -6 to 6
- top_inverse: bfloat16 [4, 4096, 4096], P('panel', 'front'), may hold values from -1 to 4
- leaf_inverse: bfloat16 [4, 2304, 256, 256], P('panel', 'front'), may hold values from -1 to 4
- boundary: bfloat16 [4, 2304, 128, 256], P('panel', 'front'), may hold values from -0.09375 to 0.09375
- touch_rows: int32 [4, 2304, 128], P('panel', 'front'), may hold values from 0 to 4095, as said below
- coupling: float32 [4, 4096], P('panel', 'front'), may hold values from 0.3 to 1
Outputs:
- top_field: bfloat16 [4, 128, 4096], P('panel', None, 'front')
- leaf_field: bfloat16 [4, 128, 589824], P('panel', None, 'front')
Inputs may be any that keep to these rules, and one draw needn't show every extreme that they name: `touch_rows`: front index d owns top front rows d * 64 to (d + 1) * 64 - 1; leaf j of a panel touches only rows owned by front indices j // 36 - 1, j // 36 and j // 36 + 1.
All inputs are finite; a program needn't handle non-finite values.
Results may differ from a plain program's by a relative error of at most 0.02.
Values may be sent and summed in bfloat16 or wider, within the bound.
A program may use at most 64 MiB of HBM per device.

v0:
```python
import jax
import jax.numpy as jnp
from jax import lax
from jax.sharding import PartitionSpec as P


def extended(value, sides, width):
    for axis, dim in sides:
        devices, length = (lax.axis_size(axis), value.shape[dim])
        up = [(i, (i + 1) % devices) for i in range(devices - 1)]
        down = [(j, i) for i, j in up]
        last = lax.slice_in_dim(value, length - width, length, axis=dim)
        leading = lax.slice_in_dim(value, 0, width, axis=dim)
        before = lax.ppermute(last, axis, up)
        after = lax.ppermute(leading, axis, down)
        value = jnp.concatenate([before, value, after], axis=dim)
    return value


def passed_along(block, axis, distance):
    devices = range(lax.axis_size(axis))
    route = [(i - distance, i) for i in devices if i - distance in devices]
    return lax.ppermute(block, axis, route)


def leaf_apply(inverse_blocks, vectors):
    return jnp.einsum("jab,sjb->sja", inverse_blocks, vectors, preferred_element_type=jnp.float32)


def top_fold(vectors, inverse_rows):
    return lax.dot_general(
        lax.all_gather(vectors, "front", axis=1, tiled=True),
        inverse_rows,
        (((1,), (1,)), ((), ())),
        preferred_element_type=jnp.float32,
    )


def lift_through(values, local_rows, boundary, leaf_inverse):
    rows_here = values.shape[2]
    window = extended(values, (("front", 2),), rows_here)
    flat_rows = local_rows[0].reshape(-1)
    picked = jnp.take(window[0], flat_rows, axis=1).reshape(
        values.shape[1], local_rows.shape[1], local_rows.shape[2]
    )
    lifted = jnp.einsum(
        "jkb,sjk->sjb", boundary[0], picked, preferred_element_type=jnp.float32
    ).astype(jnp.bfloat16)
    results = [leaf_apply(leaf_inverse[0], lifted)]
    return jnp.stack(results)


def place_wave(finished, fresh, first_row, in_range):
    older = lax.dynamic_slice_in_dim(finished, first_row, fresh.shape[1], 1)
    return lax.dynamic_update_slice_in_dim(
        finished, jnp.where(in_range, fresh, older), first_row, 1
    )


def body(top_source, leaf_source, top_inverse, leaf_inverse, boundary, touch_rows, coupling):
    panels_here = top_source.shape[0]
    sources_all = top_source.shape[1]
    rows_here = top_source.shape[2]
    leaf_count = leaf_inverse.shape[1]
    leaf_size = leaf_inverse.shape[2]
    group_count = lax.axis_size("panel")
    group_rank = lax.axis_index("panel")
    row_offset = lax.axis_index("front") * rows_here
    local_rows = touch_rows - (row_offset - rows_here)
    vectors = leaf_source.reshape(panels_here, sources_all, leaf_count, leaf_size)
    panel_index = 0
    interior_one = leaf_apply(leaf_inverse[panel_index], vectors[panel_index]).astype(jnp.bfloat16)
    pushed = jnp.einsum(
        "jkb,sjb->sjk", boundary[panel_index], interior_one, preferred_element_type=jnp.float32
    )
    window_one = jnp.zeros((sources_all, 3 * rows_here), jnp.float32)
    window_one = window_one.at[:, local_rows[panel_index].reshape(-1)].add(
        pushed.reshape(sources_all, -1)
    )
    interior_list = [interior_one]
    window_list = [window_one]
    interior = jnp.stack(interior_list)
    windows = jnp.stack(window_list)
    from_below = passed_along(
        windows[:, :, 2 * rows_here :].astype(jnp.bfloat16), "front", 1
    ).astype(jnp.float32)
    from_above = passed_along(windows[:, :, :rows_here].astype(jnp.bfloat16), "front", -1).astype(
        jnp.float32
    )
    known_part = windows[:, :, rows_here : 2 * rows_here] + from_below + from_above
    wave_count = 1
    wave_rows = sources_all // wave_count
    turn_count = group_count + wave_count - 1

    def forward_turn(turn_index, carry):
        incoming, top_done = carry
        wave_index = turn_index - group_rank
        in_range = (wave_index >= 0) & (wave_index < wave_count)
        first_row = jnp.clip(wave_index, 0, wave_count - 1) * wave_rows
        previous = incoming
        own_terms = top_source[0].astype(jnp.float32) + coupling[0] * previous.astype(jnp.float32)
        solved = top_fold((own_terms - known_part[0]).astype(jnp.bfloat16), top_inverse[0])
        previous = solved.astype(jnp.bfloat16)
        top_parts = [previous]
        top_done = place_wave(top_done, jnp.stack(top_parts), first_row, in_range)
        outgoing = passed_along(previous, "panel", 1)
        return (outgoing, top_done)

    start_edge = jnp.zeros((wave_rows, rows_here), jnp.bfloat16)
    unused_edge, forward_tops = lax.fori_loop(
        0, turn_count, forward_turn, (start_edge, jnp.zeros_like(top_source))
    )

    def backward_turn(turn_index, carry):
        incoming, top_done, fixes_done = carry
        wave_index = turn_index - (group_count - 1 - group_rank)
        in_range = (wave_index >= 0) & (wave_index < wave_count)
        first_row = jnp.clip(wave_index, 0, wave_count - 1) * wave_rows
        arriving = incoming
        top_parts = [None] * panels_here
        fix_parts = [None] * panels_here
        for panel_index in reversed(range(panels_here)):
            correction = top_fold(arriving, top_inverse[panel_index]).astype(jnp.bfloat16)
            top_new = (
                forward_tops[panel_index].astype(jnp.float32) + correction.astype(jnp.float32)
            ).astype(jnp.bfloat16)
            top_parts[panel_index] = top_new
            fix_parts[panel_index] = correction
            arriving = (coupling[panel_index] * top_new.astype(jnp.float32)).astype(jnp.bfloat16)
        top_done = place_wave(top_done, jnp.stack(top_parts), first_row, in_range)
        fixes_done = place_wave(fixes_done, jnp.stack(fix_parts), first_row, in_range)
        outgoing = passed_along(arriving, "panel", -1)
        return (outgoing, top_done, fixes_done)

    backward_state = (start_edge, jnp.zeros_like(top_source), jnp.zeros_like(top_source))
    final_edge, top_field, corrections = lax.fori_loop(0, turn_count, backward_turn, backward_state)
    forward_leaf = (
        interior.astype(jnp.float32)
        - lift_through(forward_tops, local_rows, boundary, leaf_inverse)
    ).astype(jnp.bfloat16)
    leaf_field = (
        forward_leaf.astype(jnp.float32)
        - lift_through(corrections, local_rows, boundary, leaf_inverse)
    ).astype(jnp.bfloat16)
    return (top_field, leaf_field.reshape(panels_here, sources_all, -1))


def solution(mesh):
    placed = (
        P("panel", None, "front"),
        P("panel", None, "front"),
        P("panel", "front", None),
        P("panel", "front", None, None),
        P("panel", "front", None, None),
        P("panel", "front", None),
        P("panel", "front"),
    )
    return jax.shard_map(
        body,
        mesh=mesh,
        in_specs=placed,
        out_specs=(P("panel", None, "front"), P("panel", None, "front")),
        check_vma=False,
    )
```

profile of v0, /device:TPU:1, one launch (start us, length us, event | category | flops | bytes accessed | tf_op | source)
XLA Modules:
  0.0 814.4 jit_solution(17682458878577789062)
XLA Ops:
  7.2 4.4 copy.10
  11.7 4.7 fusion.32
  16.5 2.2 fusion.19
  18.7 25.4 %scatter_custom_fusion = f32[128,192]{0,1:T(8,128)S(1)} fusion(s32[4608]{0:T(1024)S(1)} %fusion.44, f32[4608,128]{1,0:T(8,128)} %bitcast.136, f32[]{:T(128)} %constant.79.clone.1), kind=kCustom, calls=%fused_computation.44 | custom fusion | flops 589824 | bytes 98816 | tf_op jit(solution)/shard_map/scatter-add | solution.py:77
  44.1 4.9 collective-permute-start.2
  49.0 1.9 collective-permute-start.3
  51.7 2.4 collective-permute-done.3
  54.2 349.1 %while.36 = (s32[]{:T(128)}, bf16[128,64]{0,1:T(8,128)(2,1)S(1)}, bf16[1,128,64]{1,2,0:T(8,128)(2,1)}, bf16[1,128,64]{1,2,0:T(8,128)(2,1)S(1)}, f32[1,64]{1,0:T(...) while((s32[]{:T(128)}, bf16[128,64]{0,1:T(8,128)(2,1)S(1)}, ...), condition=%wide.region_2.3_spmd.clone, body=%wide.region_1.2_spmd.clone.sunk | while | flops 67182600 | bytes 4964833 | solution.py:110
  54.9 83.0 %all-gather.3.cloned.1.call-done = bf16[128,4096]{0,1:T(8,128)(2,1)} async-done(((bf16[128,64]{0,1:T(8,128)(2,1)}), bf16[128,4096]{0,1:T(8,128)(2,1)}) %all-gather.3.cloned.1.call-update) | async-done | bytes 1048592 | tf_op jit(solution)/shard_map/while/body/eval_jaxpr/all_gather | solution.py:32
  137.9 2.1 bitcast_select_fusion.5
  140.1 3.1 collective-permute-start
  144.8 79.7 %all-gather.3.cloned.1.call-done = bf16[128,4096]{0,1:T(8,128)(2,1)} async-done(((bf16[128,64]{0,1:T(8,128)(2,1)}), bf16[128,4096]{0,1:T(8,128)(2,1)}) %all-gather.3.cloned.1.call-update) | async-done | bytes 1048592 | tf_op jit(solution)/shard_map/while/body/eval_jaxpr/all_gather | solution.py:32
  224.4 2.1 bitcast_select_fusion.5
  226.6 3.1 collective-permute-start
  231.3 79.7 %all-gather.3.cloned.1.call-done = bf16[128,4096]{0,1:T(8,128)(2,1)} async-done(((bf16[128,64]{0,1:T(8,128)(2,1)}), bf16[128,4096]{0,1:T(8,128)(2,1)}) %all-gather.3.cloned.1.call-update) | async-done | bytes 1048592 | tf_op jit(solution)/shard_map/while/body/eval_jaxpr/all_gather | solution.py:32
  310.9 2.1 bitcast_select_fusion.5
  313.1 3.1 collective-permute-start
  317.7 79.4 %all-gather.3.cloned.1.call-done = bf16[128,4096]{0,1:T(8,128)(2,1)} async-done(((bf16[128,64]{0,1:T(8,128)(2,1)}), bf16[128,4096]{0,1:T(8,128)(2,1)}) %all-gather.3.cloned.1.call-update) | async-done | bytes 1048592 | tf_op jit(solution)/shard_map/while/body/eval_jaxpr/all_gather | solution.py:32
  397.1 2.1 bitcast_select_fusion.5
  399.3 3.1 collective-permute-start
  403.2 3.0 collective-permute-start.5
  406.3 2.5 collective-permute-start.4
  408.8 343.5 %while.37 = (s32[]{:T(128)}, bf16[128,64]{0,1:T(8,128)(2,1)S(1)}, bf16[1,128,64]{1,2,0:T(8,128)(2,1)S(1)}, bf16[1,128,64]{1,2,0:T(8,128)(2,1)S(1)}, f32[1,64]{1,...) while((s32[]{:T(128)}, bf16[128,64]{0,1:T(8,128)(2,1)S(1)}, ...), condition=%wide.region_4.5_spmd.clone, body=%wide.region_3.4_spmd.clone.sunk | while | flops 67239936 | bytes 5046789 | solution.py:136
  409.5 79.3 %all-gather.5.cloned.1.call-done = bf16[128,4096]{0,1:T(8,128)(2,1)} async-done(((bf16[128,64]{0,1:T(8,128)(2,1)}), bf16[128,4096]{0,1:T(8,128)(2,1)}) %all-gather.5.cloned.1.call-update) | async-done | bytes 1048592 | tf_op jit(solution)/shard_map/while/body/eval_jaxpr/all_gather | solution.py:32
  488.8 1.5 multiply_convert_fusion.2
  490.3 1.3 collective-permute-start.1
  492.4 2.4 collective-permute-done.1
  495.5 78.9 %all-gather.5.cloned.1.call-done = bf16[128,4096]{0,1:T(8,128)(2,1)} async-done(((bf16[128,64]{0,1:T(8,128)(2,1)}), bf16[128,4096]{0,1:T(8,128)(2,1)}) %all-gather.5.cloned.1.call-update) | async-done | bytes 1048592 | tf_op jit(solution)/shard_map/while/body/eval_jaxpr/all_gather | solution.py:32
  574.4 1.5 multiply_convert_fusion.2
  575.9 1.3 collective-permute-start.1
  578.0 2.4 collective-permute-done.1
  581.2 79.1 %all-gather.5.cloned.1.call-done = bf16[128,4096]{0,1:T(8,128)(2,1)} async-done(((bf16[128,64]{0,1:T(8,128)(2,1)}), bf16[128,4096]{0,1:T(8,128)(2,1)}) %all-gather.5.cloned.1.call-update) | async-done | bytes 1048592 | tf_op jit(solution)/shard_map/while/body/eval_jaxpr/all_gather | solution.py:32
  660.3 1.5 multiply_convert_fusion.2
  661.9 1.3 collective-permute-start.1
  663.9 2.4 collective-permute-done.1
  667.1 79.1 %all-gather.5.cloned.1.call-done = bf16[128,4096]{0,1:T(8,128)(2,1)} async-done(((bf16[128,64]{0,1:T(8,128)(2,1)}), bf16[128,4096]{0,1:T(8,128)(2,1)}) %all-gather.5.cloned.1.call-update) | async-done | bytes 1048592 | tf_op jit(solution)/shard_map/while/body/eval_jaxpr/all_gather | solution.py:32
  746.3 1.5 multiply_convert_fusion.2
  747.8 1.3 collective-permute-start.1
  749.8 2.4 collective-permute-done.1
  752.3 3.3 collective-permute-start.7
  755.6 2.2 collective-permute-start.6
  758.6 10.2 %gather_fusion = bf16[4608,128]{1,0:T(8,128)(2,1)} fusion(bf16[128,192]{0,1:T(8,128)(2,1)S(1)} %maximum_bitcast_fusion, s32[5120]{0:T(1024)S(1)} %pad_clamp_fusion), kind=kCustom, calls=%fused_computation.clone | custom fusion | bytes 2377728 | tf_op jit(solution)/shard_map/jit(_take)/gather | solution.py:43
  768.8 10.2 %gather_fusion.1 = bf16[4608,128]{1,0:T(8,128)(2,1)} fusion(bf16[128,192]{0,1:T(8,128)(2,1)S(1)} %maximum_bitcast_fusion.1, s32[5120]{0:T(1024)S(1)} %pad_clamp_fusion), kind=kCustom, calls=%fused_computation.1.clone | custom fusion | bytes 2377728 | tf_op jit(solution)/shard_map/jit(_take)/gather | solution.py:43
  779.0 4.7 broadcast_select_fusion.1
  783.6 7.2 fusion.7
  790.8 8.2 %fusion.5 = bf16[128,36,256]{2,0,1:T(8,128)(2,1)} fusion(f32[36,128,256]{2,1,0:T(8,128)} %fusion.7, bf16[36,128,256]{2,1,0:T(8,128)(2,1)} %copy-done.2, bf16[1,36,256,256]{3,2,1,0:T(8,128)(2,1)} %param.16, bf16[128,36,128]{0,2,1:T(8,128)(2,1)S(1)} %bitcast.134, bf16[1,36,128,256]{3,2,1,0:T(8,128)(2,1)S(1)} %copy-done), kind=kOutput, calls=%fused_computation.17 | convolution fusion | flops 914227200 | bytes 17694720 | tf_op jit(solution)/shard_map/jab,sjb->sja/dot_general | solution.py:27
  799.0 4.3 copy.12
  803.3 4.3 copy.13
  (72 shorter events, 13.5 us)
Async XLA Ops:
  7.2 9.3 %copy-start = (bf16[1,36,128,256]{3,2,1,0:T(8,128)(2,1)S(1)}, bf16[1,36,128,256]{3,2,1,0:T(8,128)(2,1)}, u32[]{:S(2)}) copy-start(bf16[1,36,128,256]{3,2,1,0:T(8,128)(2,1)} %param.17) | copy-start | bytes 7077892
  7.2 4.4 copy-start.6
  16.4 2.2 copy-start.2
  16.5 37.7 %copy-start.1 = (bf16[1,64,4096]{2,1,0:T(8,128)(2,1)S(1)}, bf16[1,64,4096]{2,1,0:T(8,128)(2,1)}, u32[]{:S(2)}) copy-start(bf16[1,64,4096]{2,1,0:T(8,128)(2,1)} %param.15) | copy-start | bytes 1572868
  16.5 37.7 %copy-start.4 = (bf16[1,128,64]{1,2,0:T(8,128)(2,1)S(1)}, bf16[1,128,64]{1,2,0:T(8,128)(2,1)}, u32[]{:S(2)}) copy-start(bf16[1,128,64]{1,2,0:T(8,128)(2,1)} %param.13) | copy-start | bytes 49156
  16.5 37.7 %copy-start.7 = (f32[1,64]{1,0:T(1,128)S(1)}, f32[1,64]{1,0:T(1,128)}, u32[]{:S(2)}) copy-start(f32[1,64]{1,0:T(1,128)} %param.19) | copy-start | bytes 772
  44.1 7.6 collective-permute-start.2
  49.0 5.1 collective-permute-start.3
  54.2 83.7 %all-gather.3.cloned.1.call-start = ((), (), s32[]{:S(2)}) async-start(), calls=%async_computation | async-start | bytes 1064960 | tf_op jit(solution)/shard_map/while/body/eval_jaxpr/all_gather | solution.py:32
  140.1 3.9 collective-permute-start
  144.0 80.4 %all-gather.3.cloned.1.call-start = ((), (), s32[]{:S(2)}) async-start(), calls=%async_computation | async-start | bytes 1064960 | tf_op jit(solution)/shard_map/while/body/eval_jaxpr/all_gather | solution.py:32
  226.6 3.9 collective-permute-start
  230.5 80.4 %all-gather.3.cloned.1.call-start = ((), (), s32[]{:S(2)}) async-start(), calls=%async_computation | async-start | bytes 1064960 | tf_op jit(solution)/shard_map/while/body/eval_jaxpr/all_gather | solution.py:32
  313.1 3.9 collective-permute-start
  317.0 80.1 %all-gather.3.cloned.1.call-start = ((), (), s32[]{:S(2)}) async-start(), calls=%async_computation | async-start | bytes 1064960 | tf_op jit(solution)/shard_map/while/body/eval_jaxpr/all_gather | solution.py:32
  399.3 3.9 collective-permute-start
  403.2 354.6 %collective-permute-start.5 = (bf16[1,128,64]{1,2,0:T(8,128)(2,1)}, bf16[1,128,64]{1,2,0:T(8,128)(2,1)S(1)}, u32[]{:S(2)}, u32[]{:S(2)}) collective-permute-start(bf16[1,128,64]{1,2,0:T(8,128)(2,1)} %get-tuple-element.580), channel_id=1, source_target_pairs={{1,0},{2,1},{3,2},{4,3},{5,4},{6,5},{7,6},{8,7},{9,8},{10,9},{11,1... | collective-permute-start | bytes 49160 | tf_op jit(solution)/shard_map/ppermute | solution.py:15
  406.3 351.6 %collective-permute-start.4 = (bf16[1,128,64]{1,2,0:T(8,128)(2,1)}, bf16[1,128,64]{1,2,0:T(8,128)(2,1)S(1)}, u32[]{:S(2)}, u32[]{:S(2)}) collective-permute-start(bf16[1,128,64]{1,2,0:T(8,128)(2,1)} %get-tuple-element.580), channel_id=1, source_target_pairs={{0,1},{1,2},{2,3},{3,4},{4,5},{5,6},{6,7},{7,8},{8,9},{9,10},{10,1... | collective-permute-start | bytes 49160 | tf_op jit(solution)/shard_map/ppermute | solution.py:14
  408.8 0.6 copy-start.3
  408.8 80.0 %all-gather.5.cloned.1.call-start = ((), (), s32[]{:S(2)}) async-start(), calls=%async_computation.1 | async-start | bytes 1064960 | tf_op jit(solution)/shard_map/while/body/eval_jaxpr/all_gather | solution.py:32
  490.3 4.5 collective-permute-start.1
  494.8 0.6 copy-start.3
  494.8 79.6 %all-gather.5.cloned.1.call-start = ((), (), s32[]{:S(2)}) async-start(), calls=%async_computation.1 | async-start | bytes 1064960 | tf_op jit(solution)/shard_map/while/body/eval_jaxpr/all_gather | solution.py:32
  575.9 4.5 collective-permute-start.1
  580.4 0.6 copy-start.3
  580.4 79.9 %all-gather.5.cloned.1.call-start = ((), (), s32[]{:S(2)}) async-start(), calls=%async_computation.1 | async-start | bytes 1064960 | tf_op jit(solution)/shard_map/while/body/eval_jaxpr/all_gather | solution.py:32
  661.9 4.5 collective-permute-start.1
  666.4 0.6 copy-start.3
  666.4 79.9 %all-gather.5.cloned.1.call-start = ((), (), s32[]{:S(2)}) async-start(), calls=%async_computation.1 | async-start | bytes 1064960 | tf_op jit(solution)/shard_map/while/body/eval_jaxpr/all_gather | solution.py:32
  747.8 4.5 collective-permute-start.1
  752.3 16.5 %copy-start.5 = (bf16[1,128,64]{1,2,0:T(8,128)(2,1)}, bf16[1,128,64]{1,2,0:T(8,128)(2,1)S(1)}, u32[]{:S(2)}) copy-start(bf16[1,128,64]{1,2,0:T(8,128)(2,1)S(1)} %get-tuple-element.391) | copy-start | bytes 49156
  752.3 16.5 %collective-permute-start.7 = (bf16[1,128,64]{1,2,0:T(8,128)(2,1)S(1)}, bf16[1,128,64]{1,2,0:T(8,128)(2,1)S(1)}, u32[]{:S(2)}, u32[]{:S(2)}) collective-permute-start(bf16[1,128,64]{1,2,0:T(8,128)(2,1)S(1)} %get-tuple-element.336), channel_id=1, source_target_pairs={{1,0},{2,1},{3,2},{4,3},{5,4},{6,5},{7,6},{8,7},{9,8},{10,9},{11,1... | collective-permute-start | bytes 49160 | tf_op jit(solution)/shard_map/ppermute | solution.py:15
  755.6 13.2 %collective-permute-start.6 = (bf16[1,128,64]{1,2,0:T(8,128)(2,1)S(1)}, bf16[1,128,64]{1,2,0:T(8,128)(2,1)S(1)}, u32[]{:S(2)}, u32[]{:S(2)}) collective-permute-start(bf16[1,128,64]{1,2,0:T(8,128)(2,1)S(1)} %get-tuple-element.336), channel_id=1, source_target_pairs={{0,1},{1,2},{2,3},{3,4},{4,5},{5,6},{6,7},{7,8},{8,9},{9,10},{10,1... | collective-permute-start | bytes 49160 | tf_op jit(solution)/shard_map/ppermute | solution.py:14
  768.8 10.2 %copy-start.8 = (pred[4608]{0:T(1024)(128)(4,1)S(1)}, pred[4608]{0:T(1024)(128)(4,1)}, u32[]{:S(2)}) copy-start(pred[4608]{0:T(1024)(128)(4,1)} %compare_and_fusion) | copy-start | bytes 13828
Sparse Core Ops, SparseCore 0:
  58.3 79.5 all-gather.2
  148.2 76.2 all-gather.2
  234.7 76.2 all-gather.2
  320.9 76.2 all-gather.2
  412.7 76.0 all-gather.4
  498.7 75.6 all-gather.4
  584.6 75.6 all-gather.4
  670.5 75.6 all-gather.4
where the time goes:
time: 816 us; the launch traced here: 814 us
  waiting for transfers between devices  654 us (80%)
  other arithmetic  37.2 us (5%)
  matrix products  37.1 us (5%)
  local copies, waits for them, and re-layouts  35.7 us (4%)
  starting transfers between devices  35.5 us (4%)
  between operations  14.3 us (2%)
    all_gather x8, waiting for transfers between devices, top_fold(): lax.all_gather(vectors, 'front', axis=1, tiled=True)  638 us
    scatter-add x1, other arithmetic, body(): window_one.at[:, local_rows[panel_index].reshape(-1)]  25.4 us
    ppermute x10, starting transfers between devices, passed_along(): return lax.ppermute(block, axis, route)  24.3 us
    gather x2, local copies, waits for them, and re-layouts, lift_through(): jnp.take(window[0], flat_rows, axis=1)  20.3 us
    dot_general x3, matrix products, leaf_apply(): jnp.einsum('jab,sjb->sja', inverse_blocks, vectors, preferred_element_typ...  20.1 us
  transfers between devices with their start and end apart: 22, of which 17 were waited for; matrix products, arithmetic and copies ran while one was open for 3% of the time, Pallas kernels for 0%

commit v1 on v0

--- a/solution.py
+++ b/solution.py
@@ -29,7 +29,9 @@
 
 def top_fold(vectors, inverse_rows):
     return lax.dot_general(
-        lax.all_gather(vectors, "front", axis=1, tiled=True),
+        jnp.concatenate(
+            lax.all_to_all(jnp.stack([vectors] * lax.axis_size("front")), "front", 0, 0), axis=1
+        ),
         inverse_rows,
         (((1,), (1,)), ((), ())),
         preferred_element_type=jnp.float32,

time: 816 us -> 460 us (0.56)
  waiting for transfers between devices: 654 us -> 245 us
  starting transfers between devices: 35.5 us -> 98.5 us
  between operations: 14.3 us -> 0.89 us
    all_gather x8 -> x0, waiting for transfers between devices: 638 us -> none  [top_fold(): lax.all_gather(vectors, 'front', axis=1, tiled=True)]
    all_to_all x0 -> x8, waiting for transfers between devices: none -> 228 us  [top_fold(): lax.all_to_all(jnp.stack([vectors] * lax.axis_size('front')), 'front', 0, 0)]
    all_to_all x0 -> x8, starting transfers between devices: none -> 60.1 us  [top_fold(): lax.all_to_all(jnp.stack([vectors] * lax.axis_size('front')), 'front', 0, 0)]
    another operation x0 -> x8, local copies, waits for them, and re-layouts: none -> 9.79 us  [top_fold(): jnp.stack([vectors] * lax.axis_size('front'))]
  transfers between devices with their start and end apart: 22 -> 22, of which waited for: 17 -> 17; matrix products, arithmetic and copies ran while one was open for 3% -> 5% of each run, Pallas kernels for 0% -> 0%
where the time goes in v1:
time: 460 us; the launch traced here: 458 us
  waiting for transfers between devices  245 us (53%)
  starting transfers between devices  98.5 us (21%)
  local copies, waits for them, and re-layouts  43.1 us (9%)
  matrix products  35.6 us (8%)
  other arithmetic  34.8 us (8%)
    all_to_all x8, waiting for transfers between devices, top_fold(): lax.all_to_all(jnp.stack([vectors] * lax.axis_size('front')), 'front', 0, 0)  228 us
    all_to_all x8, starting transfers between devices, top_fold(): lax.all_to_all(jnp.stack([vectors] * lax.axis_size('front')), 'front', 0, 0)  60.1 us
    ppermute x10, starting transfers between devices, passed_along(): return lax.ppermute(block, axis, route)  26.8 us
    scatter-add x1, other arithmetic, body(): window_one.at[:, local_rows[panel_index].reshape(-1)]  25.4 us
    gather x2, local copies, waits for them, and re-layouts, lift_through(): jnp.take(window[0], flat_rows, axis=1)  20.3 us
    dot_general x3, matrix products, leaf_apply(): jnp.einsum('jab,sjb->sja', inverse_blocks, vectors, preferred_element_typ...  20.1 us
    ppermute x10, waiting for transfers between devices, passed_along(): return lax.ppermute(block, axis, route)  16.6 us
    dot_general x8, matrix products, top_fold(): lax.dot_general(jnp.concatenate(lax.all_to_all(jnp.stack([vectors] * lax....  13.3 us
  transfers between devices with their start and end apart: 22, of which 17 were waited for; matrix products, arithmetic and copies ran while one was open for 5% of the time, Pallas kernels for 0%

profile of v1, /device:TPU:1, one launch (start us, length us, event | category | flops | bytes accessed | tf_op | source)
XLA Modules:
  0.0 458.0 jit_solution(15172391638993485842)
XLA Ops:
  0.7 4.4 copy.12
  5.1 4.7 %fusion.32 = bf16[36,128,256]{2,1,0:T(8,128)(2,1)S(1)} fusion(bf16[128,36,256]{0,2,1:T(8,128)(2,1)} %bitcast.145, bf16[1,36,256,256]{3,2,1,0:T(8,128)(2,1)} %param.16), kind=kOutput, calls=%fused_computation.37 | convolution fusion | flops 605159424 | bytes 9437184 | tf_op jit(solution)/shard_map/jab,sjb->sja/dot_general | solution.py:27
  9.9 2.2 fusion.19
  12.1 25.4 %scatter_custom_fusion = f32[128,192]{0,1:T(8,128)S(1)} fusion(s32[4608]{0:T(1024)S(1)} %fusion.44, f32[4608,128]{1,0:T(8,128)} %bitcast.148, f32[]{:T(128)} %constant.79.clone.1), kind=kCustom, calls=%fused_computation.44 | custom fusion | flops 589824 | bytes 98816 | tf_op jit(solution)/shard_map/scatter-add | solution.py:79
  37.6 4.9 %collective-permute-start.2 = (bf16[1,128,64]{1,2,0:T(8,128)(2,1)S(1)}, bf16[1,128,64]{1,2,0:T(8,128)(2,1)S(1)}, u32[]{:S(2)}, u32[]{:S(2)}) collective-permute-start(bf16[1,128,64]{1,2,0:T(8,128)(2,1)S(1)} %get-tuple-element.431), channel_id=1, source_target_pairs={{0,1},{1,2},{2,3},{3,4},{4,5},{5,6},{6,7},{7,8},{8,9},{9,10},{10,1... | collective-permute-start | bytes 49160 | tf_op jit(solution)/shard_map/ppermute | solution.py:23
  42.5 1.9 collective-permute-start.3
  45.2 2.4 collective-permute-done.3
  47.6 178.3 %while.36 = (s32[]{:T(128)}, bf16[128,64]{0,1:T(8,128)(2,1)S(1)}, bf16[1,128,64]{1,2,0:T(8,128)(2,1)}, bf16[1,128,64]{1,2,0:T(8,128)(2,1)S(1)}, f32[1,64]{1,0:T(...) while((s32[]{:T(128)}, bf16[128,64]{0,1:T(8,128)(2,1)S(1)}, ...), condition=%wide.region_2.3_spmd.clone, body=%wide.region_1.2_spmd.clone.sunk | while | flops 67182600 | bytes 5980633 | solution.py:112
  48.9 11.6 %all-to-all-start = ((bf16[64,128,64]{1,2,0:T(8,128)(2,1)}), bf16[64,128,64]{1,2,0:T(8,128)(2,1)S(1)}, u32[]{:S(2)}, u32[]{:S(2)}) async-start(bf16[64,128,64]{1,2,0:T(8,128)(2,1)} %stack.44), calls=%async_computation | async-start | bytes 2097152 | tf_op jit(solution)/shard_map/while/body/eval_jaxpr/all_to_all | solution.py:33
  60.6 28.5 %all-to-all-done = bf16[64,128,64]{1,2,0:T(8,128)(2,1)S(1)} async-done(((bf16[64,128,64]{1,2,0:T(8,128)(2,1)}), bf16[64,128,64]{1,2,0:T(8,128)(2,1)S(1)}, u32[]{:S(2)}, u32[]{:S(2)}) %all-to-all-start) | async-done | bytes 1048608 | tf_op jit(solution)/shard_map/while/body/eval_jaxpr/all_to_all | solution.py:33
  89.1 2.0 bitcast_select_fusion.5
  91.0 3.1 collective-permute-start
  96.3 7.1 %all-to-all-start = ((bf16[64,128,64]{1,2,0:T(8,128)(2,1)}), bf16[64,128,64]{1,2,0:T(8,128)(2,1)S(1)}, u32[]{:S(2)}, u32[]{:S(2)}) async-start(bf16[64,128,64]{1,2,0:T(8,128)(2,1)} %stack.44), calls=%async_computation | async-start | bytes 2097152 | tf_op jit(solution)/shard_map/while/body/eval_jaxpr/all_to_all | solution.py:33
  103.4 28.5 %all-to-all-done = bf16[64,128,64]{1,2,0:T(8,128)(2,1)S(1)} async-done(((bf16[64,128,64]{1,2,0:T(8,128)(2,1)}), bf16[64,128,64]{1,2,0:T(8,128)(2,1)S(1)}, u32[]{:S(2)}, u32[]{:S(2)}) %all-to-all-start) | async-done | bytes 1048608 | tf_op jit(solution)/shard_map/while/body/eval_jaxpr/all_to_all | solution.py:33
  131.9 2.0 bitcast_select_fusion.5
  133.9 3.9 collective-permute-start
  139.9 7.1 %all-to-all-start = ((bf16[64,128,64]{1,2,0:T(8,128)(2,1)}), bf16[64,128,64]{1,2,0:T(8,128)(2,1)S(1)}, u32[]{:S(2)}, u32[]{:S(2)}) async-start(bf16[64,128,64]{1,2,0:T(8,128)(2,1)} %stack.44), calls=%async_computation | async-start | bytes 2097152 | tf_op jit(solution)/shard_map/while/body/eval_jaxpr/all_to_all | solution.py:33
  147.0 28.5 %all-to-all-done = bf16[64,128,64]{1,2,0:T(8,128)(2,1)S(1)} async-done(((bf16[64,128,64]{1,2,0:T(8,128)(2,1)}), bf16[64,128,64]{1,2,0:T(8,128)(2,1)S(1)}, u32[]{:S(2)}, u32[]{:S(2)}) %all-to-all-start) | async-done | bytes 1048608 | tf_op jit(solution)/shard_map/while/body/eval_jaxpr/all_to_all | solution.py:33
  175.5 2.0 bitcast_select_fusion.5
  177.5 3.9 collective-permute-start
  183.6 7.1 %all-to-all-start = ((bf16[64,128,64]{1,2,0:T(8,128)(2,1)}), bf16[64,128,64]{1,2,0:T(8,128)(2,1)S(1)}, u32[]{:S(2)}, u32[]{:S(2)}) async-start(bf16[64,128,64]{1,2,0:T(8,128)(2,1)} %stack.44), calls=%async_computation | async-start | bytes 2097152 | tf_op jit(solution)/shard_map/while/body/eval_jaxpr/all_to_all | solution.py:33
  190.6 28.5 %all-to-all-done = bf16[64,128,64]{1,2,0:T(8,128)(2,1)S(1)} async-done(((bf16[64,128,64]{1,2,0:T(8,128)(2,1)}), bf16[64,128,64]{1,2,0:T(8,128)(2,1)S(1)}, u32[]{:S(2)}, u32[]{:S(2)}) %all-to-all-start) | async-done | bytes 1048608 | tf_op jit(solution)/shard_map/while/body/eval_jaxpr/all_to_all | solution.py:33
  219.1 2.0 bitcast_select_fusion.5
  221.1 3.9 collective-permute-start
  225.9 2.8 collective-permute-start.5
  228.7 2.8 collective-permute-start.4
  231.5 170.8 %while.37 = (s32[]{:T(128)}, bf16[128,64]{0,1:T(8,128)(2,1)S(1)}, bf16[1,128,64]{1,2,0:T(8,128)(2,1)S(1)}, bf16[1,128,64]{1,2,0:T(8,128)(2,1)S(1)}, f32[1,64]{1,...) while((s32[]{:T(128)}, bf16[128,64]{0,1:T(8,128)(2,1)S(1)}, ...), condition=%wide.region_4.5_spmd.clone, body=%wide.region_3.4_spmd.clone.sunk | while | flops 67239936 | bytes 5997025 | solution.py:138
  232.8 6.1 %all-to-all-start.1 = ((bf16[64,128,64]{1,2,0:T(8,128)(2,1)}), bf16[64,128,64]{1,2,0:T(8,128)(2,1)S(1)}, u32[]{:S(2)}, u32[]{:S(2)}) async-start(bf16[64,128,64]{1,2,0:T(8,128)(2,1)} %stack.45), calls=%async_computation.1 | async-start | bytes 2097152 | tf_op jit(solution)/shard_map/while/body/eval_jaxpr/all_to_all | solution.py:33
  238.9 28.5 %all-to-all-done.1 = bf16[64,128,64]{1,2,0:T(8,128)(2,1)S(1)} async-done(((bf16[64,128,64]{1,2,0:T(8,128)(2,1)}), bf16[64,128,64]{1,2,0:T(8,128)(2,1)S(1)}, u32[]{:S(2)}, u32[]{:S(2)}) %all-to-all-start.1) | async-done | bytes 1048608 | tf_op jit(solution)/shard_map/while/body/eval_jaxpr/all_to_all | solution.py:33
  270.8 2.7 collective-permute-done.1
  274.7 7.1 %all-to-all-start.1 = ((bf16[64,128,64]{1,2,0:T(8,128)(2,1)}), bf16[64,128,64]{1,2,0:T(8,128)(2,1)S(1)}, u32[]{:S(2)}, u32[]{:S(2)}) async-start(bf16[64,128,64]{1,2,0:T(8,128)(2,1)} %stack.45), calls=%async_computation.1 | async-start | bytes 2097152 | tf_op jit(solution)/shard_map/while/body/eval_jaxpr/all_to_all | solution.py:33
  281.9 28.5 %all-to-all-done.1 = bf16[64,128,64]{1,2,0:T(8,128)(2,1)S(1)} async-done(((bf16[64,128,64]{1,2,0:T(8,128)(2,1)}), bf16[64,128,64]{1,2,0:T(8,128)(2,1)S(1)}, u32[]{:S(2)}, u32[]{:S(2)}) %all-to-all-start.1) | async-done | bytes 1048608 | tf_op jit(solution)/shard_map/while/body/eval_jaxpr/all_to_all | solution.py:33
  313.8 2.7 collective-permute-done.1
  317.7 7.1 %all-to-all-start.1 = ((bf16[64,128,64]{1,2,0:T(8,128)(2,1)}), bf16[64,128,64]{1,2,0:T(8,128)(2,1)S(1)}, u32[]{:S(2)}, u32[]{:S(2)}) async-start(bf16[64,128,64]{1,2,0:T(8,128)(2,1)} %stack.45), calls=%async_computation.1 | async-start | bytes 2097152 | tf_op jit(solution)/shard_map/while/body/eval_jaxpr/all_to_all | solution.py:33
  324.8 28.5 %all-to-all-done.1 = bf16[64,128,64]{1,2,0:T(8,128)(2,1)S(1)} async-done(((bf16[64,128,64]{1,2,0:T(8,128)(2,1)}), bf16[64,128,64]{1,2,0:T(8,128)(2,1)S(1)}, u32[]{:S(2)}, u32[]{:S(2)}) %all-to-all-start.1) | async-done | bytes 1048608 | tf_op jit(solution)/shard_map/while/body/eval_jaxpr/all_to_all | solution.py:33
  356.7 2.7 collective-permute-done.1
  360.6 7.1 %all-to-all-start.1 = ((bf16[64,128,64]{1,2,0:T(8,128)(2,1)}), bf16[64,128,64]{1,2,0:T(8,128)(2,1)S(1)}, u32[]{:S(2)}, u32[]{:S(2)}) async-start(bf16[64,128,64]{1,2,0:T(8,128)(2,1)} %stack.45), calls=%async_computation.1 | async-start | bytes 2097152 | tf_op jit(solution)/shard_map/while/body/eval_jaxpr/all_to_all | solution.py:33
  367.8 28.5 %all-to-all-done.1 = bf16[64,128,64]{1,2,0:T(8,128)(2,1)S(1)} async-done(((bf16[64,128,64]{1,2,0:T(8,128)(2,1)}), bf16[64,128,64]{1,2,0:T(8,128)(2,1)S(1)}, u32[]{:S(2)}, u32[]{:S(2)}) %all-to-all-start.1) | async-done | bytes 1048608 | tf_op jit(solution)/shard_map/while/body/eval_jaxpr/all_to_all | solution.py:33
  399.7 2.7 collective-permute-done.1
  402.4 2.9 collective-permute-start.7
  405.2 3.0 collective-permute-start.6
  409.0 10.2 %gather_fusion = bf16[4608,128]{1,0:T(8,128)(2,1)} fusion(bf16[128,192]{0,1:T(8,128)(2,1)S(1)} %maximum_bitcast_fusion, s32[5120]{0:T(1024)S(1)} %pad_clamp_fusion), kind=kCustom, calls=%fused_computation.clone | custom fusion | bytes 2377728 | tf_op jit(solution)/shard_map/jit(_take)/gather | solution.py:45
  419.2 10.2 %gather_fusion.1 = bf16[4608,128]{1,0:T(8,128)(2,1)} fusion(bf16[128,192]{0,1:T(8,128)(2,1)S(1)} %maximum_bitcast_fusion.1, s32[5120]{0:T(1024)S(1)} %pad_clamp_fusion), kind=kCustom, calls=%fused_computation.1.clone | custom fusion | bytes 2377728 | tf_op jit(solution)/shard_map/jit(_take)/gather | solution.py:45
  429.4 4.7 %broadcast_select_fusion.1 = (bf16[4608,128]{1,0:T(8,128)(2,1)S(1)}, bf16[4608,128]{1,0:T(8,128)(2,1)}) fusion(bf16[4608,128]{1,0:T(8,128)(2,1)} %gather_fusion, pred[4608]{0:T(1024)(128)(4,1)S(1)} %copy-done.6, bf16[4608,128]{1,0:T(8,128)(2,1)} %gather_fusion.1), kind=kLoop, calls=%fused_computation.39 | loop fusion | flops 1179648 | bytes 4723200 | tf_op jit(solution)/shard_map/jit(_take)/select_n | solution.py:45
  434.0 7.2 %fusion.7 = f32[36,128,256]{2,1,0:T(8,128)} fusion(bf16[1,36,256,256]{3,2,1,0:T(8,128)(2,1)} %param.16, bf16[128,36,128]{0,2,1:T(8,128)(2,1)} %bitcast.147, bf16[1,36,128,256]{3,2,1,0:T(8,128)(2,1)S(1)} %copy-done), kind=kOutput, calls=%fused_computation.20 | convolution fusion | flops 907149312 | bytes 12976128 | tf_op jit(solution)/shard_map/jab,sjb->sja/dot_general | solution.py:27
  441.2 8.2 %fusion.5 = bf16[128,36,256]{2,0,1:T(8,128)(2,1)} fusion(f32[36,128,256]{2,1,0:T(8,128)} %fusion.7, bf16[36,128,256]{2,1,0:T(8,128)(2,1)} %copy-done.1, bf16[1,36,256,256]{3,2,1,0:T(8,128)(2,1)} %param.16, bf16[128,36,128]{0,2,1:T(8,128)(2,1)S(1)} %bitcast.146, bf16[1,36,128,256]{3,2,1,0:T(8,128)(2,1)S(1)} %copy-done), kind=kOutput, calls=%fused_computation.17 | convolution fusion | flops 914227200 | bytes 17694720 | tf_op jit(solution)/shard_map/jab,sjb->sja/dot_general | solution.py:27
  449.4 4.3 copy.14
  453.7 4.3 copy.15
  (62 shorter events, 28.6 us)
Async XLA Ops:
  0.6 9.3 %copy-start = (bf16[1,36,128,256]{3,2,1,0:T(8,128)(2,1)S(1)}, bf16[1,36,128,256]{3,2,1,0:T(8,128)(2,1)}, u32[]{:S(2)}) copy-start(bf16[1,36,128,256]{3,2,1,0:T(8,128)(2,1)} %param.17) | copy-start | bytes 7077892
  0.6 4.4 copy-start.4
  9.9 2.2 copy-start.1
  9.9 37.7 %copy-start.2 = (bf16[1,128,64]{1,2,0:T(8,128)(2,1)S(1)}, bf16[1,128,64]{1,2,0:T(8,128)(2,1)}, u32[]{:S(2)}) copy-start(bf16[1,128,64]{1,2,0:T(8,128)(2,1)} %param.13) | copy-start | bytes 49156
  9.9 37.7 %copy-start.5 = (f32[1,64]{1,0:T(1,128)S(1)}, f32[1,64]{1,0:T(1,128)}, u32[]{:S(2)}) copy-start(f32[1,64]{1,0:T(1,128)} %param.19) | copy-start | bytes 772
  37.6 7.6 %collective-permute-start.2 = (bf16[1,128,64]{1,2,0:T(8,128)(2,1)S(1)}, bf16[1,128,64]{1,2,0:T(8,128)(2,1)S(1)}, u32[]{:S(2)}, u32[]{:S(2)}) collective-permute-start(bf16[1,128,64]{1,2,0:T(8,128)(2,1)S(1)} %get-tuple-element.431), channel_id=1, source_target_pairs={{0,1},{1,2},{2,3},{3,4},{4,5},{5,6},{6,7},{7,8},{8,9},{9,10},{10,1... | collective-permute-start | bytes 49160 | tf_op jit(solution)/shard_map/ppermute | solution.py:23
  42.5 5.1 %collective-permute-start.3 = (bf16[1,128,64]{1,2,0:T(8,128)(2,1)S(1)}, bf16[1,128,64]{1,2,0:T(8,128)(2,1)S(1)}, u32[]{:S(2)}, u32[]{:S(2)}) collective-permute-start(bf16[1,128,64]{1,2,0:T(8,128)(2,1)S(1)} %get-tuple-element.432), channel_id=1, source_target_pairs={{1,0},{2,1},{3,2},{4,3},{5,4},{6,5},{7,6},{8,7},{9,8},{10,9},{11,1... | collective-permute-start | bytes 49160 | tf_op jit(solution)/shard_map/ppermute | solution.py:23
  48.9 40.2 %all-to-all-start = ((bf16[64,128,64]{1,2,0:T(8,128)(2,1)}), bf16[64,128,64]{1,2,0:T(8,128)(2,1)S(1)}, u32[]{:S(2)}, u32[]{:S(2)}) async-start(bf16[64,128,64]{1,2,0:T(8,128)(2,1)} %stack.44), calls=%async_computation | async-start | bytes 2097152 | tf_op jit(solution)/shard_map/while/body/eval_jaxpr/all_to_all | solution.py:33
  91.0 4.0 collective-permute-start
  96.3 35.6 %all-to-all-start = ((bf16[64,128,64]{1,2,0:T(8,128)(2,1)}), bf16[64,128,64]{1,2,0:T(8,128)(2,1)S(1)}, u32[]{:S(2)}, u32[]{:S(2)}) async-start(bf16[64,128,64]{1,2,0:T(8,128)(2,1)} %stack.44), calls=%async_computation | async-start | bytes 2097152 | tf_op jit(solution)/shard_map/while/body/eval_jaxpr/all_to_all | solution.py:33
  133.9 4.8 %collective-permute-start = (bf16[128,64]{0,1:T(8,128)(2,1)S(1)}, bf16[128,64]{0,1:T(8,128)(2,1)S(1)}, u32[]{:S(2)}, u32[]{:S(2)}) collective-permute-start(bf16[128,64]{0,1:T(8,128)(2,1)S(1)} %get-tuple-element.531), channel_id=1, source_target_pairs={{0,64},{64,128},{128,192},{1,65},{65,129},{129,193},{2,66},{66,130... | collective-permute-start | bytes 49160 | tf_op jit(solution)/shard_map/while/body/eval_jaxpr/ppermute | solution.py:23
  139.9 35.6 %all-to-all-start = ((bf16[64,128,64]{1,2,0:T(8,128)(2,1)}), bf16[64,128,64]{1,2,0:T(8,128)(2,1)S(1)}, u32[]{:S(2)}, u32[]{:S(2)}) async-start(bf16[64,128,64]{1,2,0:T(8,128)(2,1)} %stack.44), calls=%async_computation | async-start | bytes 2097152 | tf_op jit(solution)/shard_map/while/body/eval_jaxpr/all_to_all | solution.py:33
  177.5 4.8 %collective-permute-start = (bf16[128,64]{0,1:T(8,128)(2,1)S(1)}, bf16[128,64]{0,1:T(8,128)(2,1)S(1)}, u32[]{:S(2)}, u32[]{:S(2)}) collective-permute-start(bf16[128,64]{0,1:T(8,128)(2,1)S(1)} %get-tuple-element.531), channel_id=1, source_target_pairs={{0,64},{64,128},{128,192},{1,65},{65,129},{129,193},{2,66},{66,130... | collective-permute-start | bytes 49160 | tf_op jit(solution)/shard_map/while/body/eval_jaxpr/ppermute | solution.py:23
  183.6 35.6 %all-to-all-start = ((bf16[64,128,64]{1,2,0:T(8,128)(2,1)}), bf16[64,128,64]{1,2,0:T(8,128)(2,1)S(1)}, u32[]{:S(2)}, u32[]{:S(2)}) async-start(bf16[64,128,64]{1,2,0:T(8,128)(2,1)} %stack.44), calls=%async_computation | async-start | bytes 2097152 | tf_op jit(solution)/shard_map/while/body/eval_jaxpr/all_to_all | solution.py:33
  221.1 4.8 %collective-permute-start = (bf16[128,64]{0,1:T(8,128)(2,1)S(1)}, bf16[128,64]{0,1:T(8,128)(2,1)S(1)}, u32[]{:S(2)}, u32[]{:S(2)}) collective-permute-start(bf16[128,64]{0,1:T(8,128)(2,1)S(1)} %get-tuple-element.531), channel_id=1, source_target_pairs={{0,64},{64,128},{128,192},{1,65},{65,129},{129,193},{2,66},{66,130... | collective-permute-start | bytes 49160 | tf_op jit(solution)/shard_map/while/body/eval_jaxpr/ppermute | solution.py:23
  225.9 182.4 %collective-permute-start.5 = (bf16[1,128,64]{1,2,0:T(8,128)(2,1)}, bf16[1,128,64]{1,2,0:T(8,128)(2,1)S(1)}, u32[]{:S(2)}, u32[]{:S(2)}) collective-permute-start(bf16[1,128,64]{1,2,0:T(8,128)(2,1)} %get-tuple-element.580), channel_id=1, source_target_pairs={{1,0},{2,1},{3,2},{4,3},{5,4},{6,5},{7,6},{8,7},{9,8},{10,9},{11,1... | collective-permute-start | bytes 49160 | tf_op jit(solution)/shard_map/ppermute | solution.py:15
  228.7 179.5 %collective-permute-start.4 = (bf16[1,128,64]{1,2,0:T(8,128)(2,1)}, bf16[1,128,64]{1,2,0:T(8,128)(2,1)S(1)}, u32[]{:S(2)}, u32[]{:S(2)}) collective-permute-start(bf16[1,128,64]{1,2,0:T(8,128)(2,1)} %get-tuple-element.580), channel_id=1, source_target_pairs={{0,1},{1,2},{2,3},{3,4},{4,5},{5,6},{6,7},{7,8},{8,9},{9,10},{10,1... | collective-permute-start | bytes 49160 | tf_op jit(solution)/shard_map/ppermute | solution.py:14
  232.8 34.6 %all-to-all-start.1 = ((bf16[64,128,64]{1,2,0:T(8,128)(2,1)}), bf16[64,128,64]{1,2,0:T(8,128)(2,1)S(1)}, u32[]{:S(2)}, u32[]{:S(2)}) async-start(bf16[64,128,64]{1,2,0:T(8,128)(2,1)} %stack.45), calls=%async_computation.1 | async-start | bytes 2097152 | tf_op jit(solution)/shard_map/while/body/eval_jaxpr/all_to_all | solution.py:33
  268.8 4.7 %collective-permute-start.1 = (bf16[128,64]{0,1:T(8,128)(2,1)S(1)}, bf16[128,64]{0,1:T(8,128)(2,1)S(1)}, u32[]{:S(2)}, u32[]{:S(2)}) collective-permute-start(bf16[128,64]{0,1:T(8,128)(2,1)S(1)} %get-tuple-element.541), channel_id=1, source_target_pairs={{64,0},{128,64},{192,128},{65,1},{129,65},{193,129},{66,2},{130,66... | collective-permute-start | bytes 49160 | tf_op jit(solution)/shard_map/while/body/eval_jaxpr/ppermute | solution.py:23
  274.7 35.6 %all-to-all-start.1 = ((bf16[64,128,64]{1,2,0:T(8,128)(2,1)}), bf16[64,128,64]{1,2,0:T(8,128)(2,1)S(1)}, u32[]{:S(2)}, u32[]{:S(2)}) async-start(bf16[64,128,64]{1,2,0:T(8,128)(2,1)} %stack.45), calls=%async_computation.1 | async-start | bytes 2097152 | tf_op jit(solution)/shard_map/while/body/eval_jaxpr/all_to_all | solution.py:33
  311.7 4.7 %collective-permute-start.1 = (bf16[128,64]{0,1:T(8,128)(2,1)S(1)}, bf16[128,64]{0,1:T(8,128)(2,1)S(1)}, u32[]{:S(2)}, u32[]{:S(2)}) collective-permute-start(bf16[128,64]{0,1:T(8,128)(2,1)S(1)} %get-tuple-element.541), channel_id=1, source_target_pairs={{64,0},{128,64},{192,128},{65,1},{129,65},{193,129},{66,2},{130,66... | collective-permute-start | bytes 49160 | tf_op jit(solution)/shard_map/while/body/eval_jaxpr/ppermute | solution.py:23
  317.7 35.6 %all-to-all-start.1 = ((bf16[64,128,64]{1,2,0:T(8,128)(2,1)}), bf16[64,128,64]{1,2,0:T(8,128)(2,1)S(1)}, u32[]{:S(2)}, u32[]{:S(2)}) async-start(bf16[64,128,64]{1,2,0:T(8,128)(2,1)} %stack.45), calls=%async_computation.1 | async-start | bytes 2097152 | tf_op jit(solution)/shard_map/while/body/eval_jaxpr/all_to_all | solution.py:33
  354.7 4.7 %collective-permute-start.1 = (bf16[128,64]{0,1:T(8,128)(2,1)S(1)}, bf16[128,64]{0,1:T(8,128)(2,1)S(1)}, u32[]{:S(2)}, u32[]{:S(2)}) collective-permute-start(bf16[128,64]{0,1:T(8,128)(2,1)S(1)} %get-tuple-element.541), channel_id=1, source_target_pairs={{64,0},{128,64},{192,128},{65,1},{129,65},{193,129},{66,2},{130,66... | collective-permute-start | bytes 49160 | tf_op jit(solution)/shard_map/while/body/eval_jaxpr/ppermute | solution.py:23
  360.6 35.6 %all-to-all-start.1 = ((bf16[64,128,64]{1,2,0:T(8,128)(2,1)}), bf16[64,128,64]{1,2,0:T(8,128)(2,1)S(1)}, u32[]{:S(2)}, u32[]{:S(2)}) async-start(bf16[64,128,64]{1,2,0:T(8,128)(2,1)} %stack.45), calls=%async_computation.1 | async-start | bytes 2097152 | tf_op jit(solution)/shard_map/while/body/eval_jaxpr/all_to_all | solution.py:33
  397.6 4.7 %collective-permute-start.1 = (bf16[128,64]{0,1:T(8,128)(2,1)S(1)}, bf16[128,64]{0,1:T(8,128)(2,1)S(1)}, u32[]{:S(2)}, u32[]{:S(2)}) collective-permute-start(bf16[128,64]{0,1:T(8,128)(2,1)S(1)} %get-tuple-element.541), channel_id=1, source_target_pairs={{64,0},{128,64},{192,128},{65,1},{129,65},{193,129},{66,2},{130,66... | collective-permute-start | bytes 49160 | tf_op jit(solution)/shard_map/while/body/eval_jaxpr/ppermute | solution.py:23
  402.4 16.8 %copy-start.3 = (bf16[1,128,64]{1,2,0:T(8,128)(2,1)}, bf16[1,128,64]{1,2,0:T(8,128)(2,1)S(1)}, u32[]{:S(2)}) copy-start(bf16[1,128,64]{1,2,0:T(8,128)(2,1)S(1)} %get-tuple-element.391) | copy-start | bytes 49156
  402.4 16.8 %collective-permute-start.7 = (bf16[1,128,64]{1,2,0:T(8,128)(2,1)S(1)}, bf16[1,128,64]{1,2,0:T(8,128)(2,1)S(1)}, u32[]{:S(2)}, u32[]{:S(2)}) collective-permute-start(bf16[1,128,64]{1,2,0:T(8,128)(2,1)S(1)} %get-tuple-element.336), channel_id=1, source_target_pairs={{1,0},{2,1},{3,2},{4,3},{5,4},{6,5},{7,6},{8,7},{9,8},{10,9},{11,1... | collective-permute-start | bytes 49160 | tf_op jit(solution)/shard_map/ppermute | solution.py:15
  405.2 13.9 %collective-permute-start.6 = (bf16[1,128,64]{1,2,0:T(8,128)(2,1)S(1)}, bf16[1,128,64]{1,2,0:T(8,128)(2,1)S(1)}, u32[]{:S(2)}, u32[]{:S(2)}) collective-permute-start(bf16[1,128,64]{1,2,0:T(8,128)(2,1)S(1)} %get-tuple-element.336), channel_id=1, source_target_pairs={{0,1},{1,2},{2,3},{3,4},{4,5},{5,6},{6,7},{7,8},{8,9},{9,10},{10,1... | collective-permute-start | bytes 49160 | tf_op jit(solution)/shard_map/ppermute | solution.py:14
  419.2 10.2 %copy-start.6 = (pred[4608]{0:T(1024)(128)(4,1)S(1)}, pred[4608]{0:T(1024)(128)(4,1)}, u32[]{:S(2)}) copy-start(pred[4608]{0:T(1024)(128)(4,1)} %compare_and_fusion) | copy-start | bytes 13828
